TPU v7x, 128 devices: a whole 4x4x4 slice. The times are simulated.
128 devices in a mesh: grp: 2 (over y_lo), dev: 64 (over y_hi, x, z, core).
Axes of the slice: x: 4, y: 4 (y_hi: 2, y_lo: 2; y = y_hi * 2 + y_lo), z: 4, core: 2. Of those that a mesh axis runs over, the one named last changes fastest.
Arguments:
- weights: float32 [2, 64, 524288], P(None, None, ('grp', 'dev')), may hold values from -3 to 3
- owner_map: int32 [16], replicated, may hold values from 0 to 15, each once
- node_index: int32 [2, 64], replicated, may hold values from 0 to 7, as said below
Outputs:
- transformed: float32 [2, 64, 524288], P(None, None, ('grp', 'dev'))
Inputs may be any that keep to these rules, and one draw needn't show every extreme that they name: owner_map[col] = 2 k + rx puts coarse frequency column col at column slot rx of device group k, in grp+dev order, after the middle level; every value appears once. The 64 columns (node_index[0, t], node_index[1, t]) are distinct, so every pair of Chebyshev point numbers appears once.
All inputs are finite; a program needn't handle non-finite values.
Results may differ from a plain program's by a relative error of at most 0.0003.
Values sent between devices are 32-bit elements; how exact they have to be, the bound alone decides.
A program may use at most 128 MiB of HBM per device.

v0:
```python
import math
import jax
import jax.numpy as jnp
from jax import lax
from jax.sharding import PartitionSpec as P

NFREQ = 4096
CHEB = 8
TWO_PI = 2.0 * math.pi
HIGHEST = lax.Precision.HIGHEST


def from_partner(array, axis, bit):
    return lax.ppermute(array, axis, [(i, i ^ 1 << bit) for i in range(lax.axis_size(axis))])


def cheb_points():
    counter = jnp.arange(CHEB, dtype=jnp.float32)
    return 0.5 * jnp.cos(math.pi * (2.0 * counter + 1.0) / (2.0 * CHEB))


def node_select(node_index):
    numbers = jnp.arange(CHEB, dtype=jnp.int32)[None, :]
    select_x = (node_index[0][:, None] == numbers).astype(jnp.float32)
    select_y = (node_index[1][:, None] == numbers).astype(jnp.float32)
    return (select_x, select_y)


def node_offsets(node_index):
    points = cheb_points()
    select_x, select_y = node_select(node_index)
    return (
        jnp.sum(select_x * points[None, :], axis=1),
        jnp.sum(select_y * points[None, :], axis=1),
    )


def lagrange(places):
    points = cheb_points()
    rows_out = []
    for first_id in range(CHEB):
        product = jnp.ones_like(places)
        for other_id in range(CHEB):
            if other_id != first_id:
                product = (
                    product * (places - points[other_id]) / (points[first_id] - points[other_id])
                )
        rows_out.append(product)
    return jnp.stack(rows_out)


def child_tables(node_index):
    select_x, select_y = node_select(node_index)
    offset_x, offset_y = node_offsets(node_index)
    tables = []
    for child_id in range(4):
        basis_x = lagrange(0.5 * offset_x + 0.5 * (child_id % 2) - 0.25)
        basis_y = lagrange(0.5 * offset_y + 0.5 * (child_id // 2) - 0.25)
        table_x = jnp.sum(select_x[:, :, None] * basis_x[None, :, :], axis=1)
        table_y = jnp.sum(select_y[:, :, None] * basis_y[None, :, :], axis=1)
        tables.append(table_x * table_y)
    return jnp.stack(tables)


def speeds(place_x, place_y):
    speed_one = (2.0 + jnp.sin(TWO_PI * place_x) * jnp.sin(TWO_PI * place_y)) / 16.0
    speed_two = (2.0 + jnp.cos(TWO_PI * place_x) * jnp.cos(TWO_PI * place_y)) / 16.0
    return (speed_one * speed_one, speed_two * speed_two)


def radius(speed_x, speed_y, freq_x, freq_y):
    return jnp.sqrt(speed_x * freq_x * freq_x + speed_y * freq_y * freq_y + 1.0)


def freq_phase(place_x, place_y, freq_x, freq_y, centre_x, centre_y):
    speed_x, speed_y = speeds(place_x, place_y)
    numer_part = speed_x * (freq_x - centre_x) * (freq_x + centre_x) + speed_y * (
        freq_y - centre_y
    ) * (freq_y + centre_y)
    denom_part = radius(speed_x, speed_y, freq_x, freq_y) + radius(
        speed_x, speed_y, centre_x, centre_y
    )
    return TWO_PI * (
        place_x * (freq_x - centre_x) + place_y * (freq_y - centre_y) + numer_part / denom_part
    )


def space_phase(place_x, place_y, anchor_x, anchor_y, freq_x, freq_y):
    speed_x, speed_y = speeds(place_x, place_y)
    base_x, base_y = speeds(anchor_x, anchor_y)
    numer_part = (speed_x - base_x) * freq_x * freq_x + (speed_y - base_y) * freq_y * freq_y
    denom_part = radius(speed_x, speed_y, freq_x, freq_y) + radius(base_x, base_y, freq_x, freq_y)
    return TWO_PI * (
        (place_x - anchor_x) * freq_x + (place_y - anchor_y) * freq_y + numer_part / denom_part
    )


def rotate(values, phase_angle):
    cosine = jnp.cos(phase_angle)
    sine_part = jnp.sin(phase_angle)
    return jnp.stack(
        [values[0] * cosine - values[1] * sine_part, values[0] * sine_part + values[1] * cosine]
    )


def freq_level(pieces, space_x, space_y, box_x, box_y, level_id, offset_x, offset_y):
    width_a = 2.0 ** (-level_id)
    width_b = 2.0**level_id
    half_span = 0.5 * NFREQ
    centre_ax = ((space_x + 0.5) * width_a)[None, :]
    centre_ay = ((space_y + 0.5) * width_a)[None, :]
    centre_bx = ((box_x + 0.5) * width_b - half_span)[None, :]
    centre_by = ((box_y + 0.5) * width_b - half_span)[None, :]
    running = None
    for values, child_x, child_y, table_now in pieces:
        kid_x = ((2.0 * box_x + child_x + 0.5) * (0.5 * width_b) - half_span)[
            None, :
        ] + 0.5 * width_b * offset_x[:, None]
        kid_y = ((2.0 * box_y + child_y + 0.5) * (0.5 * width_b) - half_span)[
            None, :
        ] + 0.5 * width_b * offset_y[:, None]
        phase_angle = freq_phase(centre_ax, centre_ay, kid_x, kid_y, centre_bx, centre_by)
        product_term = jnp.einsum(
            "ts,rsn->rtn", table_now, rotate(values, -phase_angle), precision=HIGHEST
        )
        running = product_term if running is None else running + product_term
    node_x = centre_bx + width_b * offset_x[:, None]
    node_y = centre_by + width_b * offset_y[:, None]
    return rotate(running, freq_phase(centre_ax, centre_ay, node_x, node_y, centre_bx, centre_by))


def space_in(values, offset_x, offset_y, parent_x, parent_y, box_x, box_y, level_id):
    width_p = 2.0 ** (1 - level_id)
    anchor_x = ((parent_x + 0.5) * width_p)[None, :]
    anchor_y = ((parent_y + 0.5) * width_p)[None, :]
    freq_x = ((box_x + 0.5) * 2.0**level_id - 0.5 * NFREQ)[None, :]
    freq_y = ((box_y + 0.5) * 2.0**level_id - 0.5 * NFREQ)[None, :]
    place_x = anchor_x + width_p * offset_x[:, None]
    place_y = anchor_y + width_p * offset_y[:, None]
    return rotate(values, -space_phase(place_x, place_y, anchor_x, anchor_y, freq_x, freq_y))


def space_out(
    turned_in,
    table_now,
    offset_x,
    offset_y,
    parent_x,
    parent_y,
    child_x,
    child_y,
    box_x,
    box_y,
    level_id,
):
    width_a = 2.0 ** (-level_id)
    mixed_state = jnp.einsum("st,rsn->rtn", table_now, turned_in, precision=HIGHEST)
    anchor_x = ((parent_x + 0.5) * 2.0 * width_a)[None, :]
    anchor_y = ((parent_y + 0.5) * 2.0 * width_a)[None, :]
    place_x = ((2.0 * parent_x + child_x + 0.5) * width_a)[None, :] + width_a * offset_x[:, None]
    place_y = ((2.0 * parent_y + child_y + 0.5) * width_a)[None, :] + width_a * offset_y[:, None]
    freq_x = ((box_x + 0.5) * 2.0**level_id - 0.5 * NFREQ)[None, :]
    freq_y = ((box_y + 0.5) * 2.0**level_id - 0.5 * NFREQ)[None, :]
    return rotate(mixed_state, space_phase(place_x, place_y, anchor_x, anchor_y, freq_x, freq_y))


def first_geometry(step_id, group_ids, low_digit, high_digit, loc_ids, across):
    column = loc_ids % across
    row_id = loc_ids // across
    if step_id == 0:
        space_x = 2 * group_ids + low_digit % 2
        space_y = low_digit // 2
        box_x = 2 * column + high_digit % 2
        box_y = 2 * row_id + high_digit // 2
    else:
        space_x = 4 * group_ids + 2 * (low_digit % 2) + high_digit % 2
        space_y = 2 * (low_digit // 2) + high_digit // 2
        box_x = column
        box_y = row_id
    return [
        jnp.broadcast_to(jnp.asarray(entry_value), loc_ids.shape).astype(jnp.float32)
        for entry_value in (space_x, space_y, box_x, box_y)
    ]


def post_layout(loc_ids, per_source, rest_rows):
    source = loc_ids // per_source
    remain = loc_ids % per_source
    rest_x = remain // rest_rows
    rest_y = remain % rest_rows
    src_group = source // 16
    src_digits = source % 16
    low_digit = src_digits % 4
    high_digit = src_digits // 4
    middle_x = 4 * src_group + 2 * (low_digit % 2) + high_digit % 2
    middle_y = 2 * (low_digit // 2) + high_digit // 2
    return (middle_x, middle_y, rest_x, rest_y)


def second_geometry(step_id, middle_x, middle_y, column, rest_y, other_digit):
    if step_id == 0:
        parent_x = middle_x
        parent_y = middle_y
        box_x = 2 * column + other_digit % 2
        box_y = 2 * rest_y + other_digit // 2
    else:
        parent_x = 2 * middle_x + other_digit % 2
        parent_y = 2 * middle_y + other_digit // 2
        box_x = column
        box_y = rest_y
    return [
        jnp.asarray(entry_value).astype(jnp.float32)
        for entry_value in (parent_x, parent_y, box_x, box_y)
    ]


def owner_inverse(owner_map, count):
    counter = jnp.arange(count, dtype=jnp.int32)
    return jnp.sum(jnp.where(owner_map[None, :] == counter[:, None], counter[None, :], 0), axis=1)


def finish_levels(pair_state, owner_map, tables, offset_x, offset_y, first_level, across):
    node_count = pair_state.shape[1]
    per_dev = pair_state.shape[2]
    dev_count = lax.axis_size("dev")
    grp_count = lax.axis_size("grp")
    devices = dev_count * grp_count
    groups = devices // 16
    per_source = per_dev // devices
    rest_rows = per_dev // across // 4
    group_width = across // 4 // groups
    grp_index = lax.axis_index("grp")
    dev_index = lax.axis_index("dev")
    flat_index = grp_index * dev_count + dev_index
    own_group = flat_index // 16
    own_digits = flat_index % 16
    loc_index = jnp.arange(per_dev, dtype=jnp.int32)
    inverse = owner_inverse(owner_map, 16)
    blocks = pair_state.reshape(2, node_count, rest_rows, 2, 2, 16, 2, 2)
    blocks = jnp.transpose(blocks, (0, 1, 5, 3, 6, 4, 7, 2))
    blocks = jnp.take(blocks, inverse, axis=2)
    blocks = blocks.reshape(2, node_count, groups, group_width, 2, 2, 2, 2, rest_rows)
    blocks = jnp.transpose(blocks, (0, 1, 2, 4, 5, 6, 7, 3, 8))
    pair_state = lax.all_to_all(
        blocks.reshape(2, node_count, devices, per_source),
        ("grp", "dev"),
        split_axis=2,
        concat_axis=2,
        tiled=True,
    ).reshape(2, node_count, per_dev)
    middle_x, middle_y, rest_x, rest_y = post_layout(loc_index, per_source, rest_rows)
    column = jnp.take(inverse, own_group * group_width + rest_x)
    for step_id in range(2):
        if step_id == 0:
            own_digit = own_digits % 4
            other_digit = own_digits // 4
        else:
            own_digit = own_digits // 4
            other_digit = own_digits % 4
        level_id = first_level + 3 + step_id
        geometry = second_geometry(step_id, middle_x, middle_y, column, rest_y, other_digit)
        pair_sum = pair_state + from_partner(pair_state, "dev", 2 * step_id)
        summed = pair_sum + from_partner(pair_sum, "dev", 2 * step_id + 1)
        turned_in = space_in(
            summed, offset_x, offset_y, geometry[0], geometry[1], geometry[2], geometry[3], level_id
        )
        table_own = lax.dynamic_index_in_dim(tables, own_digit, 0, keepdims=False)
        pair_state = space_out(
            turned_in,
            table_own,
            offset_x,
            offset_y,
            geometry[0],
            geometry[1],
            (own_digit % 2).astype(jnp.float32),
            (own_digit // 2).astype(jnp.float32),
            geometry[2],
            geometry[3],
            level_id,
        )
    return pair_state


def body(weights, owner_map, node_index):
    per_dev = weights.shape[2]
    dev_count = lax.axis_size("dev")
    levels = NFREQ.bit_length() - 1
    first_level = levels // 2 - 2
    across = 2 ** (levels // 2)
    offset_x, offset_y = node_offsets(node_index)
    tables = child_tables(node_index)
    grp_index = lax.axis_index("grp")
    dev_index = lax.axis_index("dev")
    flat_index = grp_index * dev_count + dev_index
    own_group = flat_index // 16
    own_digits = flat_index % 16
    loc_index = jnp.arange(per_dev, dtype=jnp.int32)
    pair_state = weights
    for step_id in range(2):
        if step_id == 0:
            own_digit = own_digits % 4
            low_digit = own_digit
            high_digit = own_digits // 4
        else:
            own_digit = own_digits // 4
            low_digit = own_digits % 4
            high_digit = own_digit
        near_state = from_partner(pair_state, "dev", 2 * step_id)
        far_one, far_two = from_partner((pair_state, near_state), "dev", 2 * step_id + 1)
        arrived = [pair_state, near_state, far_one, far_two]
        pieces = []
        for delta_id in range(4):
            child_id = jnp.bitwise_xor(own_digit, delta_id)
            pieces.append(
                (
                    arrived[delta_id],
                    (child_id % 2).astype(jnp.float32),
                    (child_id // 2).astype(jnp.float32),
                    lax.dynamic_index_in_dim(tables, child_id, 0, keepdims=False),
                )
            )
        geometry = first_geometry(step_id, own_group, low_digit, high_digit, loc_index, across)
        pair_state = freq_level(
            pieces,
            geometry[0],
            geometry[1],
            geometry[2],
            geometry[3],
            first_level + 1 + step_id,
            offset_x,
            offset_y,
        )
    pair_state = finish_levels(
        pair_state, owner_map, tables, offset_x, offset_y, first_level, across
    )
    return pair_state


def solution(mesh):
    in_specs = (P(None, None, ("grp", "dev")), P(), P())
    out_specs = P(None, None, ("grp", "dev"))
    return jax.shard_map(body, mesh=mesh, in_specs=in_specs, out_specs=out_specs, check_vma=False)
```

profile of v0, /device:TPU:0, one launch (start us, length us, event | category | flops | bytes accessed | tf_op | source)
XLA Modules:
  0.0 573.0 jit_solution(9209224539109127543)
XLA Ops:
  0.0 2.0 collective-permute-start.1
  2.4 0.7 fusion.459
  73.5 0.8 slice_bitcast_fusion
  74.3 4.4 divide_bitcast_fusion
  78.8 0.7 fusion.419
  79.4 0.7 fusion.433
  80.4 0.7 fusion.426
  81.2 0.7 fusion.440
  83.6 6.3 %multiply_subtract_fusion.13 = (f32[1,64,4096]{2,1,0:T(8,128)S(1)}, f32[1,64,4096]{2,1,0:T(8,128)S(1)}) fusion(f32[2,64,4096]{2,1,0:T(8,128)} %param.3, f32[4096]{0:T(1024)S(1)} %get-tuple-element.154, f32[]{:T(128)S(6)} %mul.7297, f32[]{:T(128)S(6)} %mul.7291, f32[4096]{0:T(1024)S(1)} %fusion.362, f32[64]{0:T(128)S(1)} %get-tuple-element.115, ...), kind=kLoop, calls=%fused_computation.399 | loop fusion | flops 8126464 | bytes 4276752 | tf_op jit(solution)/shard_map/sub | solution.py:102
  90.0 2.0 fusion.2
  92.5 5.1 multiply_subtract_fusion.12
  97.6 2.0 convolution_add_fusion.5
  99.6 6.8 %multiply_subtract_fusion.11 = (f32[1,64,4096]{2,1,0:T(8,128)S(1)}, f32[1,64,4096]{2,1,0:T(8,128)S(1)}) fusion(f32[2,64,4096]{2,1,0:T(8,128)} %collective-permute-done.1, f32[4096]{0:T(1024)S(1)} %get-tuple-element.154, f32[]{:T(128)S(6)} %mul.7297, f32[]{:T(128)S(6)} %mul.7291, f32[4096]{0:T(1024)S(1)} %fusion.362, f32[64]{0:T(128)S(1)} %get-tuple-element.115, ...), kind=kLoop, calls=%fused_computation.395 | loop fusion | flops 8126464 | bytes 4276752 | tf_op jit(solution)/shard_map/sub | solution.py:102
  106.5 2.0 convolution_add_fusion.4
  108.5 31.6 %collective-permute-done.2 = f32[2,64,4096]{2,1,0:T(8,128)S(1)} collective-permute-done((f32[2,64,4096]{2,1,0:T(8,128)S(1)}, f32[2,64,4096]{2,1,0:T(8,128)S(1)}, u32[]{:S(2)}, u32[]{:S(2)}) %collective-permute-start.2) | collective-permute-done | bytes 2097184 | tf_op jit(solution)/shard_map/ppermute | solution.py:14
  140.2 5.1 multiply_subtract_fusion.10
  145.2 2.0 fusion.1
  147.3 10.1 %multiply_subtract_fusion.8 = (f32[1,64,4096]{2,1,0:T(8,128)S(1)}, f32[1,64,4096]{2,1,0:T(8,128)S(1)}, f32[1,64,4096]{2,1,0:T(8,128)S(1)}) fusion(f32[4096]{0:T(1024)S(1)} %get-tuple-element.195, f32[]{:T(128)S(6)} %mul.7617, f32[]{:T(128)S(6)} %mul.7611, f32[4096]{0:T(1024)S(1)} %get-tuple-element.194, f32[64]{0:T(128)S(1)} %get-tuple-element.114, ...), kind=kLoop, calls=%fused_computation.389 | loop fusion | flops 15204352 | bytes 5374496 | tf_op jit(solution)/shard_map/sub | solution.py:102
  157.4 1.5 pad_maximum_fusion
  158.9 3.6 collective-permute-start.3
  162.5 1.5 collective-permute-start.4
  164.2 43.7 %collective-permute-done.3 = f32[2,64,4096]{2,1,0:T(8,128)} collective-permute-done((f32[2,64,4096]{2,1,0:T(8,128)}, f32[2,64,4096]{2,1,0:T(8,128)}, u32[]{:S(2)}, u32[]{:S(2)}) %collective-permute-start.3) | collective-permute-done | bytes 2097184 | tf_op jit(solution)/shard_map/ppermute | solution.py:14
  207.9 1.5 collective-permute-start.5
  209.5 6.3 %multiply_subtract_fusion.7 = (f32[1,64,4096]{2,1,0:T(8,128)S(1)}, f32[1,64,4096]{2,1,0:T(8,128)S(1)}) fusion(f32[2,64,4096]{2,1,0:T(8,128)} %collective-permute-done.3, f32[4096]{0:T(1024)S(1)} %get-tuple-element.195, f32[]{:T(128)S(6)} %mul.7617, f32[]{:T(128)S(6)} %mul.7611, f32[4096]{0:T(1024)S(1)} %get-tuple-element.194, f32[64]{0:T(128)S(1)} %get-tuple-element.114, ...), kind=kLoop, calls=%fused_computation.387 | loop fusion | flops 8126464 | bytes 4276752 | tf_op jit(solution)/shard_map/sub | solution.py:102
  215.8 6.3 %multiply_subtract_fusion.6 = (f32[1,64,4096]{2,1,0:T(8,128)S(1)}, f32[1,64,4096]{2,1,0:T(8,128)S(1)}) fusion(f32[2,64,4096]{2,1,0:T(8,128)} %collective-permute-done.4, f32[4096]{0:T(1024)S(1)} %get-tuple-element.195, f32[]{:T(128)S(6)} %mul.7617, f32[]{:T(128)S(6)} %mul.7611, f32[4096]{0:T(1024)S(1)} %get-tuple-element.194, f32[64]{0:T(128)S(1)} %get-tuple-element.114, ...), kind=kLoop, calls=%fused_computation.385 | loop fusion | flops 8126464 | bytes 4276752 | tf_op jit(solution)/shard_map/sub | solution.py:102
  222.1 32.4 %collective-permute-done.5 = f32[2,64,4096]{2,1,0:T(8,128)} collective-permute-done((f32[2,64,4096]{2,1,0:T(8,128)}, f32[2,64,4096]{2,1,0:T(8,128)}, u32[]{:S(2)}, u32[]{:S(2)}) %collective-permute-start.5) | collective-permute-done | bytes 2097184 | tf_op jit(solution)/shard_map/ppermute | solution.py:14
  254.6 11.4 %multiply_subtract_fusion.5 = (f32[1,64,4096]{2,1,0:T(8,128)S(1)}, f32[1,64,4096]{2,1,0:T(8,128)S(1)}, f32[1,64,4096]{2,1,0:T(8,128)S(1)}) fusion(f32[2,64,4096]{2,1,0:T(8,128)} %collective-permute-done.5, f32[4096]{0:T(1024)S(1)} %get-tuple-element.195, f32[]{:T(128)S(6)} %mul.7617, f32[]{:T(128)S(6)} %mul.7611, f32[4096]{0:T(1024)S(1)} %get-tuple-element.194, ...), kind=kLoop, calls=%fused_computation.383 | loop fusion | flops 15466496 | bytes 7455248 | tf_op jit(solution)/shard_map/sub | solution.py:102
  266.0 2.0 fusion.15
  268.0 2.0 convolution_add_fusion.2
  270.1 2.0 convolution_add_fusion.1
  272.1 2.0 fusion
  274.2 6.4 %multiply_subtract_fusion.4 = (f32[1,64,4096]{2,1,0:T(8,128)}, f32[1,64,4096]{2,1,0:T(8,128)S(1)}) fusion(f32[2,64,4096]{2,1,0:T(8,128)S(1)} %fusion, f32[4096]{0:T(1024)S(1)} %get-tuple-element.195, f32[]{:T(128)S(6)} %mul.7617, f32[]{:T(128)S(6)} %mul.7611, f32[64]{0:T(128)S(1)} %get-tuple-element.116, f32[4096]{0:T(1024)S(1)} %get-tuple-element.194, ...), kind=kLoop, calls=%fused_computation.381 | loop fusion | flops 7864320 | bytes 4243984 | tf_op jit(solution)/shard_map/sub | solution.py:102
  280.5 1.8 copy.29
  282.4 2.5 copy.31
  284.9 0.6 copy.30
  285.5 1.2 copy.32
  287.1 2.5 maximum_bitcast_fusion
  289.6 5.0 gather_fusion
  294.6 2.9 copy_select_fusion
  297.4 2.6 copy.46
  300.0 4.6 reshape.12153
  304.6 40.3 %all_to_all.5 = f32[128,1,4096]{2,1,0:T(1,128)} all-to-all(f32[128,1,4096]{2,1,0:T(1,128)S(1)} %reshape.12153), channel_id=1, replica_groups=mesh['grp'=2,'dev'=64] {'grp','dev'}, dimensions={0} | all-to-all | bytes 4194304 | tf_op jit(solution)/shard_map/all_to_all | solution.py:244
  345.4 7.3 %reduce.18 = f32[128,4096]{1,0:T(8,128)S(1)} reduce(f32[128,1,4096]{2,1,0:T(1,128)} %all_to_all.5, f32[]{:T(128)} %broadcast.18834), dimensions={1}, to_apply=%all_to_all.3.reduce_sub_computation | reduce | bytes 4194308 | tf_op jit(solution)/shard_map/all_to_all | solution.py:244
  352.7 3.0 reshape.12154
  355.7 4.7 copy.35
  360.4 2.8 copy.37
  363.3 4.1 collective-permute-done.6
  367.8 0.9 collective-permute-start.7
  369.8 0.7 fusion.458
  370.7 4.5 compare_select_fusion.1
  375.2 5.7 multiply_add_fusion.16
  381.2 34.5 %collective-permute-done.7 = f32[2,64,4096]{2,1,0:T(8,128)S(1)} collective-permute-done((f32[2,64,4096]{2,1,0:T(8,128)S(1)}, f32[2,64,4096]{2,1,0:T(8,128)S(1)}, u32[]{:S(2)}, u32[]{:S(2)}) %collective-permute-start.7) | collective-permute-done | bytes 2097184 | tf_op jit(solution)/shard_map/ppermute | solution.py:14
  416.0 13.1 %multiply_subtract_fusion.3 = (f32[1,64,4096]{2,1,0:T(8,128)S(1)}, f32[1,64,4096]{2,1,0:T(8,128)S(1)}) fusion(f32[2,64,4096]{2,1,0:T(8,128)S(1)} %add.5384, f32[4096]{0:T(1024)S(1)} %get-tuple-element.13, f32[4096]{0:T(1024)S(1)} %get-tuple-element.203, f32[4096]{0:T(1024)S(1)} %get-tuple-element.204, f32[4096]{0:T(1024)S(1)} %get-tuple-element.158, ...), kind=kLoop, calls=%fused_computation.379 | loop fusion | flops 10747904 | bytes 4309504 | tf_op jit(solution)/shard_map/sub | solution.py:102
  429.1 2.0 convolution_bitcast_fusion.1
  431.1 12.9 %multiply_subtract_fusion.2 = (f32[1,64,4096]{2,1,0:T(8,128)S(1)}, f32[1,64,4096]{2,1,0:T(8,128)S(1)}) fusion(f32[2,64,4096]{2,1,0:T(8,128)S(1)} %convolution_bitcast_fusion.1, f32[4096]{0:T(1024)S(1)} %get-tuple-element.13, f32[4096]{0:T(1024)S(1)} %get-tuple-element.203, f32[4096]{0:T(1024)S(1)} %get-tuple-element.204, f32[4096]{0:T(1024)S(1)} %get-tuple-element.158, ...), kind=kLoop, calls=%fused_computation.377 | loop fusion | flops 10485760 | bytes 4342272 | tf_op jit(solution)/shard_map/sub | solution.py:102
  444.1 0.8 collective-permute-start.8
  444.9 47.6 %collective-permute-done.8 = f32[2,64,4096]{2,1,0:T(8,128)S(1)} collective-permute-done((f32[2,64,4096]{2,1,0:T(8,128)S(1)}, f32[2,64,4096]{2,1,0:T(8,128)S(1)}, u32[]{:S(2)}, u32[]{:S(2)}) %collective-permute-start.8) | collective-permute-done | bytes 2097184 | tf_op jit(solution)/shard_map/ppermute | solution.py:14
  492.5 1.8 fusion.457
  495.0 46.0 %collective-permute-done.9 = f32[2,64,4096]{2,1,0:T(8,128)} collective-permute-done((f32[2,64,4096]{2,1,0:T(8,128)}, f32[2,64,4096]{2,1,0:T(8,128)}, u32[]{:S(2)}, u32[]{:S(2)}) %collective-permute-start.9) | collective-permute-done | bytes 2097184 | tf_op jit(solution)/shard_map/ppermute | solution.py:14
  541.0 2.5 fusion.460
  543.5 13.1 %multiply_subtract_fusion.1 = (f32[1,64,4096]{2,1,0:T(8,128)S(1)}, f32[1,64,4096]{2,1,0:T(8,128)S(1)}) fusion(f32[2,64,4096]{2,1,0:T(8,128)S(1)} %fusion.460, f32[4096]{0:T(1024)S(1)} %get-tuple-element.87, f32[4096]{0:T(1024)S(1)} %get-tuple-element.152, f32[4096]{0:T(1024)S(1)} %get-tuple-element.153, f32[4096]{0:T(1024)S(1)} %multiply_add_fusion.14, ...), kind=kLoop, calls=%fused_computation.375 | loop fusion | flops 10747904 | bytes 4309504 | tf_op jit(solution)/shard_map/sub | solution.py:102
  556.6 2.0 convolution_bitcast_fusion
  558.6 12.9 %multiply_subtract_fusion = (f32[2,64,4096]{2,1,0:T(8,128)S(1)}, f32[2,64,4096]{2,1,0:T(8,128)S(1)}) fusion(f32[2,64,4096]{2,1,0:T(8,128)S(1)} %convolution_bitcast_fusion, f32[4096]{0:T(1024)S(1)} %get-tuple-element.87, f32[4096]{0:T(1024)S(1)} %get-tuple-element.152, ...), kind=kLoop, output_to_operand_aliasing={{0}: (12, {}), {1}: (12, {})}, calls=%fused_computation.373 | loop fusion | flops 10485760 | bytes 4342784 | tf_op jit(solution)/shard_map/sub | solution.py:102
  571.5 1.3 copy-done.3
  (92 shorter events, 6.5 us)
Async XLA Ops:
  0.0 92.0 %collective-permute-start = (f32[2,64,4096]{2,1,0:T(8,128)}, f32[2,64,4096]{2,1,0:T(8,128)S(1)}, u32[]{:S(2)}, u32[]{:S(2)}) collective-permute-start(f32[2,64,4096]{2,1,0:T(8,128)} %param.3), channel_id=1, source_target_pairs={{0,1},{1,0},{2,3},{3,2},{4,5},{5,4},{6,7},{7,6},{8,9},{9,8},{10,11... | collective-permute-start | bytes 6291464 | tf_op jit(solution)/shard_map/ppermute | solution.py:14
  0.0 99.6 %collective-permute-start.1 = (f32[2,64,4096]{2,1,0:T(8,128)}, f32[2,64,4096]{2,1,0:T(8,128)}, u32[]{:S(2)}, u32[]{:S(2)}) collective-permute-start(f32[2,64,4096]{2,1,0:T(8,128)} %param.3), channel_id=1, source_target_pairs={{0,2},{1,3},{2,0},{3,1},{4,6},{5,7},{6,4},{7,5},{8,10},{9,11},{10,... | collective-permute-start | bytes 6291464 | tf_op jit(solution)/shard_map/ppermute | solution.py:14
  92.0 48.1 %collective-permute-start.2 = (f32[2,64,4096]{2,1,0:T(8,128)S(1)}, f32[2,64,4096]{2,1,0:T(8,128)S(1)}, u32[]{:S(2)}, u32[]{:S(2)}) collective-permute-start(f32[2,64,4096]{2,1,0:T(8,128)S(1)} %collective-permute-done), channel_id=1, source_target_pairs={{0,2},{1,3},{2,0},{3,1},{4,6},{5,7},{6,4},{7,5},{8,10},{9,11},{10,... | collective-permute-start | bytes 6291464 | tf_op jit(solution)/shard_map/ppermute | solution.py:14
  157.4 6.6 %copy-start.4 = (s32[16]{0:T(128)S(1)}, s32[16]{0:T(128)}, u32[]{:S(2)}) copy-start(s32[16]{0:T(128)} %param.4) | copy-start | bytes 196
  158.9 49.1 %collective-permute-start.3 = (f32[2,64,4096]{2,1,0:T(8,128)}, f32[2,64,4096]{2,1,0:T(8,128)}, u32[]{:S(2)}, u32[]{:S(2)}) collective-permute-start(f32[2,64,4096]{2,1,0:T(8,128)} %pad_maximum_fusion), channel_id=1, source_target_pairs={{0,4},{1,5},{2,6},{3,7},{4,0},{5,1},{6,2},{7,3},{8,12},{9,13},{10,... | collective-permute-start | bytes 6291464 | tf_op jit(solution)/shard_map/ppermute | solution.py:14
  162.5 53.3 %collective-permute-start.4 = (f32[2,64,4096]{2,1,0:T(8,128)}, f32[2,64,4096]{2,1,0:T(8,128)}, u32[]{:S(2)}, u32[]{:S(2)}) collective-permute-start(f32[2,64,4096]{2,1,0:T(8,128)} %pad_maximum_fusion), channel_id=1, source_target_pairs={{0,8},{1,9},{2,10},{3,11},{4,12},{5,13},{6,14},{7,15},{8,0},{9,1},... | collective-permute-start | bytes 6291464 | tf_op jit(solution)/shard_map/ppermute | solution.py:14
  207.9 46.6 %collective-permute-start.5 = (f32[2,64,4096]{2,1,0:T(8,128)}, f32[2,64,4096]{2,1,0:T(8,128)}, u32[]{:S(2)}, u32[]{:S(2)}) collective-permute-start(f32[2,64,4096]{2,1,0:T(8,128)} %collective-permute-done.3), channel_id=1, source_target_pairs={{0,8},{1,9},{2,10},{3,11},{4,12},{5,13},{6,14},{7,15},{8,0},{9,1},... | collective-permute-start | bytes 6291464 | tf_op jit(solution)/shard_map/ppermute | solution.py:14
  285.5 1.6 copy-start.1
  363.2 4.2 collective-permute-start.6
  367.8 48.0 %collective-permute-start.7 = (f32[2,64,4096]{2,1,0:T(8,128)S(1)}, f32[2,64,4096]{2,1,0:T(8,128)S(1)}, u32[]{:S(2)}, u32[]{:S(2)}) collective-permute-start(f32[2,64,4096]{2,1,0:T(8,128)S(1)} %add.5383), channel_id=1, source_target_pairs={{0,2},{1,3},{2,0},{3,1},{4,6},{5,7},{6,4},{7,5},{8,10},{9,11},{10,... | collective-permute-start | bytes 6291464 | tf_op jit(solution)/shard_map/ppermute | solution.py:14
  444.1 48.4 %collective-permute-start.8 = (f32[2,64,4096]{2,1,0:T(8,128)S(1)}, f32[2,64,4096]{2,1,0:T(8,128)S(1)}, u32[]{:S(2)}, u32[]{:S(2)}) collective-permute-start(f32[2,64,4096]{2,1,0:T(8,128)S(1)} %pad_maximum_fusion.1), channel_id=1, source_target_pairs={{0,4},{1,5},{2,6},{3,7},{4,0},{5,1},{6,2},{7,3},{8,12},{9,13},{10,... | collective-permute-start | bytes 6291464 | tf_op jit(solution)/shard_map/ppermute | solution.py:14
  492.5 2.0 copy-start
  494.5 46.5 %collective-permute-start.9 = (f32[2,64,4096]{2,1,0:T(8,128)}, f32[2,64,4096]{2,1,0:T(8,128)}, u32[]{:S(2)}, u32[]{:S(2)}) collective-permute-start(f32[2,64,4096]{2,1,0:T(8,128)} %fusion.457), channel_id=1, source_target_pairs={{0,8},{1,9},{2,10},{3,11},{4,12},{5,13},{6,14},{7,15},{8,0},{9,1},... | collective-permute-start | bytes 6291464 | tf_op jit(solution)/shard_map/ppermute | solution.py:14
  556.6 2.0 copy-start.2
  571.5 1.3 copy-start.3
where the time goes:
time: 580 us; the launch traced here: 573 us
  waiting for transfers between devices  240 us (41%)
  other arithmetic  156 us (27%)
  between operations  72 us (12%)
  blocking collectives  40.3 us (7%)
  local copies, waits for them, and re-layouts  33.8 us (6%)
  matrix products  20.4 us (4%)
  starting transfers between devices  11 us (2%)
    ppermute x10, waiting for transfers between devices, from_partner(): lax.ppermute(array, axis, [(i, i ^ 1 << bit) for i in range(lax.axis_size...  240 us
    sub x14, other arithmetic, rotate(): values[0] * cosine - values[1] * sine_part  116 us
    all_to_all x1, blocking collectives, finish_levels(): lax.all_to_all(blocks.reshape(2, node_count, devices, per_source), ('grp'...  40.3 us
    dot_general x8, matrix products, freq_level(): jnp.einsum('ts,rsn->rtn', table_now, rotate(values, -phase_angle), precis...  16.4 us
  transfers between devices with their start and end apart: 10, of which 7 were waited for; matrix products, arithmetic and copies ran while one was open for 11% of the time, Pallas kernels for 0%

commit v1 on v0

--- a/solution.py
+++ b/solution.py
@@ -8,6 +8,18 @@
 CHEB = 8
 TWO_PI = 2.0 * math.pi
 HIGHEST = lax.Precision.HIGHEST
+
+
+def unit_keep_up(state):
+    return jnp.concatenate(
+        lax.all_to_all(
+            jnp.stack(jnp.split(state, lax.axis_size(("grp", "dev")), axis=2), 0),
+            ("grp", "dev"),
+            0,
+            0,
+        ),
+        2,
+    )
 
 
 def from_partner(array, axis, bit):
@@ -241,13 +253,9 @@
     blocks = jnp.take(blocks, inverse, axis=2)
     blocks = blocks.reshape(2, node_count, groups, group_width, 2, 2, 2, 2, rest_rows)
     blocks = jnp.transpose(blocks, (0, 1, 2, 4, 5, 6, 7, 3, 8))
-    pair_state = lax.all_to_all(
-        blocks.reshape(2, node_count, devices, per_source),
-        ("grp", "dev"),
-        split_axis=2,
-        concat_axis=2,
-        tiled=True,
-    ).reshape(2, node_count, per_dev)
+    pair_state = unit_keep_up(blocks.reshape(2, node_count, devices, per_source)).reshape(
+        2, node_count, per_dev
+    )
     middle_x, middle_y, rest_x, rest_y = post_layout(loc_index, per_source, rest_rows)
     column = jnp.take(inverse, own_group * group_width + rest_x)
     for step_id in range(2):

time: 580 us -> 581 us (level)
    unnamed x12 -> x141, local copies, waits for them, and re-layouts: 9.48 us -> 13.2 us
  transfers between devices with their start and end apart: 10 -> 10, of which waited for: 7 -> 7; matrix products, arithmetic and copies ran while one was open for 11% -> 10% of each run, Pallas kernels for 0% -> 0%
where the time goes in v1:
time: 581 us; the launch traced here: 574 us
  waiting for transfers between devices  240 us (41%)
  other arithmetic  155 us (27%)
  between operations  72 us (12%)
  blocking collectives  40.2 us (7%)
  local copies, waits for them, and re-layouts  35.3 us (6%)
  matrix products  20.4 us (4%)
  starting transfers between devices  11 us (2%)
    ppermute x10, waiting for transfers between devices, from_partner(): lax.ppermute(array, axis, [(i, i ^ 1 << bit) for i in range(lax.axis_size...  240 us
    sub x14, other arithmetic, rotate(): values[0] * cosine - values[1] * sine_part  116 us
    all_to_all x1, blocking collectives, unit_keep_up(): lax.all_to_all(jnp.stack(jnp.split(state, lax.axis_size(('grp', 'dev')),...  40.2 us
    dot_general x8, matrix products, freq_level(): jnp.einsum('ts,rsn->rtn', table_now, rotate(values, -phase_angle), precis...  16.4 us
    unnamed x141, local copies, waits for them, and re-layouts  13.2 us
  transfers between devices with their start and end apart: 10, of which 7 were waited for; matrix products, arithmetic and copies ran while one was open for 10% of the time, Pallas kernels for 0%

profile of v1, /device:TPU:0, one launch (start us, length us, event | category | flops | bytes accessed | tf_op | source)
XLA Modules:
  0.0 574.3 jit_solution(2637410982830784652)
XLA Ops:
  0.0 2.0 collective-permute-start.1
  2.4 0.7 fusion.459
  72.4 0.8 slice_bitcast_fusion.128
  73.3 4.4 divide_bitcast_fusion
  77.7 0.6 fusion.419
  78.3 0.6 fusion.433
  80.1 0.6 fusion.440
  82.5 6.3 %multiply_subtract_fusion.13 = (f32[1,64,4096]{2,1,0:T(8,128)S(1)}, f32[1,64,4096]{2,1,0:T(8,128)S(1)}) fusion(f32[2,64,4096]{2,1,0:T(8,128)} %param.3, f32[4096]{0:T(1024)S(1)} %get-tuple-element.154, f32[]{:T(128)S(6)} %mul.7297, f32[]{:T(128)S(6)} %mul.7291, f32[4096]{0:T(1024)S(1)} %fusion.362, f32[64]{0:T(128)S(1)} %get-tuple-element.115, ...), kind=kLoop, calls=%fused_computation.399 | loop fusion | flops 8126464 | bytes 4276752 | tf_op jit(solution)/shard_map/sub | solution.py:114
  88.8 2.0 fusion.2
  91.3 5.1 multiply_subtract_fusion.12
  96.4 2.0 convolution_add_fusion.5
  98.5 6.8 %multiply_subtract_fusion.11 = (f32[1,64,4096]{2,1,0:T(8,128)S(1)}, f32[1,64,4096]{2,1,0:T(8,128)S(1)}) fusion(f32[2,64,4096]{2,1,0:T(8,128)} %collective-permute-done.1, f32[4096]{0:T(1024)S(1)} %get-tuple-element.154, f32[]{:T(128)S(6)} %mul.7297, f32[]{:T(128)S(6)} %mul.7291, f32[4096]{0:T(1024)S(1)} %fusion.362, f32[64]{0:T(128)S(1)} %get-tuple-element.115, ...), kind=kLoop, calls=%fused_computation.395 | loop fusion | flops 8126464 | bytes 4276752 | tf_op jit(solution)/shard_map/sub | solution.py:114
  105.3 2.0 convolution_add_fusion.4
  107.4 31.6 %collective-permute-done.2 = f32[2,64,4096]{2,1,0:T(8,128)S(1)} collective-permute-done((f32[2,64,4096]{2,1,0:T(8,128)S(1)}, f32[2,64,4096]{2,1,0:T(8,128)S(1)}, u32[]{:S(2)}, u32[]{:S(2)}) %collective-permute-start.2) | collective-permute-done | bytes 2097184 | tf_op jit(solution)/shard_map/ppermute | solution.py:26
  139.0 5.1 multiply_subtract_fusion.10
  144.0 2.0 fusion.1
  146.1 10.1 %multiply_subtract_fusion.8 = (f32[1,64,4096]{2,1,0:T(8,128)S(1)}, f32[1,64,4096]{2,1,0:T(8,128)S(1)}, f32[1,64,4096]{2,1,0:T(8,128)S(1)}) fusion(f32[4096]{0:T(1024)S(1)} %get-tuple-element.195, f32[]{:T(128)S(6)} %mul.7617, f32[]{:T(128)S(6)} %mul.7611, f32[4096]{0:T(1024)S(1)} %get-tuple-element.194, f32[64]{0:T(128)S(1)} %get-tuple-element.114, ...), kind=kLoop, calls=%fused_computation.389 | loop fusion | flops 15204352 | bytes 5374496 | tf_op jit(solution)/shard_map/sub | solution.py:114
  156.2 1.5 pad_maximum_fusion
  157.7 3.6 collective-permute-start.3
  161.3 1.5 collective-permute-start.4
  163.1 43.7 %collective-permute-done.3 = f32[2,64,4096]{2,1,0:T(8,128)} collective-permute-done((f32[2,64,4096]{2,1,0:T(8,128)}, f32[2,64,4096]{2,1,0:T(8,128)}, u32[]{:S(2)}, u32[]{:S(2)}) %collective-permute-start.3) | collective-permute-done | bytes 2097184 | tf_op jit(solution)/shard_map/ppermute | solution.py:26
  206.8 1.5 collective-permute-start.5
  208.3 6.3 %multiply_subtract_fusion.7 = (f32[1,64,4096]{2,1,0:T(8,128)S(1)}, f32[1,64,4096]{2,1,0:T(8,128)S(1)}) fusion(f32[2,64,4096]{2,1,0:T(8,128)} %collective-permute-done.3, f32[4096]{0:T(1024)S(1)} %get-tuple-element.195, f32[]{:T(128)S(6)} %mul.7617, f32[]{:T(128)S(6)} %mul.7611, f32[4096]{0:T(1024)S(1)} %get-tuple-element.194, f32[64]{0:T(128)S(1)} %get-tuple-element.114, ...), kind=kLoop, calls=%fused_computation.387 | loop fusion | flops 8126464 | bytes 4276752 | tf_op jit(solution)/shard_map/sub | solution.py:114
  214.6 6.3 %multiply_subtract_fusion.6 = (f32[1,64,4096]{2,1,0:T(8,128)S(1)}, f32[1,64,4096]{2,1,0:T(8,128)S(1)}) fusion(f32[2,64,4096]{2,1,0:T(8,128)} %collective-permute-done.4, f32[4096]{0:T(1024)S(1)} %get-tuple-element.195, f32[]{:T(128)S(6)} %mul.7617, f32[]{:T(128)S(6)} %mul.7611, f32[4096]{0:T(1024)S(1)} %get-tuple-element.194, f32[64]{0:T(128)S(1)} %get-tuple-element.114, ...), kind=kLoop, calls=%fused_computation.385 | loop fusion | flops 8126464 | bytes 4276752 | tf_op jit(solution)/shard_map/sub | solution.py:114
  221.0 32.4 %collective-permute-done.5 = f32[2,64,4096]{2,1,0:T(8,128)} collective-permute-done((f32[2,64,4096]{2,1,0:T(8,128)}, f32[2,64,4096]{2,1,0:T(8,128)}, u32[]{:S(2)}, u32[]{:S(2)}) %collective-permute-start.5) | collective-permute-done | bytes 2097184 | tf_op jit(solution)/shard_map/ppermute | solution.py:26
  253.4 11.4 %multiply_subtract_fusion.5 = (f32[1,64,4096]{2,1,0:T(8,128)S(1)}, f32[1,64,4096]{2,1,0:T(8,128)S(1)}, f32[1,64,4096]{2,1,0:T(8,128)S(1)}) fusion(f32[2,64,4096]{2,1,0:T(8,128)} %collective-permute-done.5, f32[4096]{0:T(1024)S(1)} %get-tuple-element.195, f32[]{:T(128)S(6)} %mul.7617, f32[]{:T(128)S(6)} %mul.7611, f32[4096]{0:T(1024)S(1)} %get-tuple-element.194, ...), kind=kLoop, calls=%fused_computation.383 | loop fusion | flops 15466496 | bytes 7455248 | tf_op jit(solution)/shard_map/sub | solution.py:114
  264.8 2.0 fusion.15
  266.8 2.0 convolution_add_fusion.2
  268.9 2.0 convolution_add_fusion.1
  271.0 2.0 fusion
  273.0 6.4 %multiply_subtract_fusion.4 = (f32[1,64,4096]{2,1,0:T(8,128)}, f32[1,64,4096]{2,1,0:T(8,128)S(1)}) fusion(f32[2,64,4096]{2,1,0:T(8,128)S(1)} %fusion, f32[4096]{0:T(1024)S(1)} %get-tuple-element.195, f32[]{:T(128)S(6)} %mul.7617, f32[]{:T(128)S(6)} %mul.7611, f32[64]{0:T(128)S(1)} %get-tuple-element.116, f32[4096]{0:T(1024)S(1)} %get-tuple-element.194, ...), kind=kLoop, calls=%fused_computation.381 | loop fusion | flops 7864320 | bytes 4243984 | tf_op jit(solution)/shard_map/sub | solution.py:114
  279.4 1.8 copy.273
  281.2 2.5 copy.275
  284.4 1.2 copy.276
  286.0 2.5 maximum_bitcast_fusion
  288.4 5.0 gather_fusion
  293.4 2.9 copy_select_fusion
  298.0 1.9 copy-done.2
  299.9 4.6 reshape.12153
  304.5 40.2 %all_to_all.5 = f32[128,1,4096]{2,1,0:T(1,128)} all-to-all(f32[128,1,4096]{2,1,0:T(1,128)S(1)} %reshape.12153), channel_id=1, replica_groups=mesh['grp'=2,'dev'=64] {'grp','dev'}, dimensions={0} | all-to-all | bytes 4194304 | tf_op jit(solution)/shard_map/all_to_all | solution.py:15
  345.3 7.3 %reduce.18 = f32[128,4096]{1,0:T(8,128)S(1)} reduce(f32[128,1,4096]{2,1,0:T(1,128)} %all_to_all.5, f32[]{:T(128)} %broadcast.18834), dimensions={1}, to_apply=%all_to_all.3.reduce_sub_computation | reduce | bytes 4194308 | tf_op jit(solution)/shard_map/all_to_all | solution.py:15
  352.6 3.0 reshape.12154
  355.6 2.6 bitcast_bitcast_fusion
  358.2 2.5 copy.405
  360.7 2.8 copy.407
  363.7 4.1 collective-permute-done.6
  368.1 0.9 collective-permute-start.7
  370.1 0.7 fusion.458
  371.0 4.5 compare_select_fusion.1
  375.5 5.6 multiply_add_fusion.16
  381.5 34.5 %collective-permute-done.7 = f32[2,64,4096]{2,1,0:T(8,128)S(1)} collective-permute-done((f32[2,64,4096]{2,1,0:T(8,128)S(1)}, f32[2,64,4096]{2,1,0:T(8,128)S(1)}, u32[]{:S(2)}, u32[]{:S(2)}) %collective-permute-start.7) | collective-permute-done | bytes 2097184 | tf_op jit(solution)/shard_map/ppermute | solution.py:26
  416.3 13.1 %multiply_subtract_fusion.3 = (f32[1,64,4096]{2,1,0:T(8,128)S(1)}, f32[1,64,4096]{2,1,0:T(8,128)S(1)}) fusion(f32[2,64,4096]{2,1,0:T(8,128)S(1)} %add.5384, f32[4096]{0:T(1024)S(1)} %get-tuple-element.13, f32[4096]{0:T(1024)S(1)} %get-tuple-element.203, f32[4096]{0:T(1024)S(1)} %get-tuple-element.204, f32[4096]{0:T(1024)S(1)} %get-tuple-element.158, ...), kind=kLoop, calls=%fused_computation.379 | loop fusion | flops 10747904 | bytes 4309504 | tf_op jit(solution)/shard_map/sub | solution.py:114
  429.4 2.0 convolution_bitcast_fusion.1
  431.4 12.9 %multiply_subtract_fusion.2 = (f32[1,64,4096]{2,1,0:T(8,128)S(1)}, f32[1,64,4096]{2,1,0:T(8,128)S(1)}) fusion(f32[2,64,4096]{2,1,0:T(8,128)S(1)} %convolution_bitcast_fusion.1, f32[4096]{0:T(1024)S(1)} %get-tuple-element.13, f32[4096]{0:T(1024)S(1)} %get-tuple-element.203, f32[4096]{0:T(1024)S(1)} %get-tuple-element.204, f32[4096]{0:T(1024)S(1)} %get-tuple-element.158, ...), kind=kLoop, calls=%fused_computation.377 | loop fusion | flops 10485760 | bytes 4342272 | tf_op jit(solution)/shard_map/sub | solution.py:114
  444.4 0.8 collective-permute-start.8
  445.2 47.6 %collective-permute-done.8 = f32[2,64,4096]{2,1,0:T(8,128)S(1)} collective-permute-done((f32[2,64,4096]{2,1,0:T(8,128)S(1)}, f32[2,64,4096]{2,1,0:T(8,128)S(1)}, u32[]{:S(2)}, u32[]{:S(2)}) %collective-permute-start.8) | collective-permute-done | bytes 2097184 | tf_op jit(solution)/shard_map/ppermute | solution.py:26
  492.8 1.3 copy-done
  494.2 1.6 fusion.457
  496.2 46.0 %collective-permute-done.9 = f32[2,64,4096]{2,1,0:T(8,128)} collective-permute-done((f32[2,64,4096]{2,1,0:T(8,128)}, f32[2,64,4096]{2,1,0:T(8,128)}, u32[]{:S(2)}, u32[]{:S(2)}) %collective-permute-start.9) | collective-permute-done | bytes 2097184 | tf_op jit(solution)/shard_map/ppermute | solution.py:26
  542.2 2.5 fusion.460
  544.8 13.1 %multiply_subtract_fusion.1 = (f32[1,64,4096]{2,1,0:T(8,128)S(1)}, f32[1,64,4096]{2,1,0:T(8,128)S(1)}) fusion(f32[2,64,4096]{2,1,0:T(8,128)S(1)} %fusion.460, f32[4096]{0:T(1024)S(1)} %get-tuple-element.87, f32[4096]{0:T(1024)S(1)} %get-tuple-element.152, f32[4096]{0:T(1024)S(1)} %get-tuple-element.153, f32[4096]{0:T(1024)S(1)} %multiply_add_fusion.14, ...), kind=kLoop, calls=%fused_computation.375 | loop fusion | flops 10747904 | bytes 4309504 | tf_op jit(solution)/shard_map/sub | solution.py:114
  557.9 2.0 convolution_bitcast_fusion
  559.9 12.9 %multiply_subtract_fusion = (f32[2,64,4096]{2,1,0:T(8,128)S(1)}, f32[2,64,4096]{2,1,0:T(8,128)S(1)}) fusion(f32[2,64,4096]{2,1,0:T(8,128)S(1)} %convolution_bitcast_fusion, f32[4096]{0:T(1024)S(1)} %get-tuple-element.87, f32[4096]{0:T(1024)S(1)} %get-tuple-element.152, ...), kind=kLoop, output_to_operand_aliasing={{0}: (12, {}), {1}: (12, {})}, calls=%fused_computation.373 | loop fusion | flops 10485760 | bytes 4342784 | tf_op jit(solution)/shard_map/sub | solution.py:114
  572.8 1.3 copy-done.4
  (222 shorter events, 8.2 us)
Async XLA Ops:
  0.0 90.8 %collective-permute-start = (f32[2,64,4096]{2,1,0:T(8,128)}, f32[2,64,4096]{2,1,0:T(8,128)S(1)}, u32[]{:S(2)}, u32[]{:S(2)}) collective-permute-start(f32[2,64,4096]{2,1,0:T(8,128)} %param.3), channel_id=1, source_target_pairs={{0,1},{1,0},{2,3},{3,2},{4,5},{5,4},{6,7},{7,6},{8,9},{9,8},{10,11... | collective-permute-start | bytes 6291464 | tf_op jit(solution)/shard_map/ppermute | solution.py:26
  0.0 98.4 %collective-permute-start.1 = (f32[2,64,4096]{2,1,0:T(8,128)}, f32[2,64,4096]{2,1,0:T(8,128)}, u32[]{:S(2)}, u32[]{:S(2)}) collective-permute-start(f32[2,64,4096]{2,1,0:T(8,128)} %param.3), channel_id=1, source_target_pairs={{0,2},{1,3},{2,0},{3,1},{4,6},{5,7},{6,4},{7,5},{8,10},{9,11},{10,... | collective-permute-start | bytes 6291464 | tf_op jit(solution)/shard_map/ppermute | solution.py:26
  90.8 48.1 %collective-permute-start.2 = (f32[2,64,4096]{2,1,0:T(8,128)S(1)}, f32[2,64,4096]{2,1,0:T(8,128)S(1)}, u32[]{:S(2)}, u32[]{:S(2)}) collective-permute-start(f32[2,64,4096]{2,1,0:T(8,128)S(1)} %collective-permute-done), channel_id=1, source_target_pairs={{0,2},{1,3},{2,0},{3,1},{4,6},{5,7},{6,4},{7,5},{8,10},{9,11},{10,... | collective-permute-start | bytes 6291464 | tf_op jit(solution)/shard_map/ppermute | solution.py:26
  146.1 16.7 %copy-start.5 = (s32[16]{0:T(128)S(1)}, s32[16]{0:T(128)}, u32[]{:S(2)}) copy-start(s32[16]{0:T(128)} %param.4) | copy-start | bytes 196
  157.7 49.1 %collective-permute-start.3 = (f32[2,64,4096]{2,1,0:T(8,128)}, f32[2,64,4096]{2,1,0:T(8,128)}, u32[]{:S(2)}, u32[]{:S(2)}) collective-permute-start(f32[2,64,4096]{2,1,0:T(8,128)} %pad_maximum_fusion), channel_id=1, source_target_pairs={{0,4},{1,5},{2,6},{3,7},{4,0},{5,1},{6,2},{7,3},{8,12},{9,13},{10,... | collective-permute-start | bytes 6291464 | tf_op jit(solution)/shard_map/ppermute | solution.py:26
  161.3 53.3 %collective-permute-start.4 = (f32[2,64,4096]{2,1,0:T(8,128)}, f32[2,64,4096]{2,1,0:T(8,128)}, u32[]{:S(2)}, u32[]{:S(2)}) collective-permute-start(f32[2,64,4096]{2,1,0:T(8,128)} %pad_maximum_fusion), channel_id=1, source_target_pairs={{0,8},{1,9},{2,10},{3,11},{4,12},{5,13},{6,14},{7,15},{8,0},{9,1},... | collective-permute-start | bytes 6291464 | tf_op jit(solution)/shard_map/ppermute | solution.py:26
  206.8 46.6 %collective-permute-start.5 = (f32[2,64,4096]{2,1,0:T(8,128)}, f32[2,64,4096]{2,1,0:T(8,128)}, u32[]{:S(2)}, u32[]{:S(2)}) collective-permute-start(f32[2,64,4096]{2,1,0:T(8,128)} %collective-permute-done.3), channel_id=1, source_target_pairs={{0,8},{1,9},{2,10},{3,11},{4,12},{5,13},{6,14},{7,15},{8,0},{9,1},... | collective-permute-start | bytes 6291464 | tf_op jit(solution)/shard_map/ppermute | solution.py:26
  284.4 1.6 copy-start.1
  298.0 1.9 copy-start.2
  363.6 4.2 collective-permute-start.6
  368.1 48.0 %collective-permute-start.7 = (f32[2,64,4096]{2,1,0:T(8,128)S(1)}, f32[2,64,4096]{2,1,0:T(8,128)S(1)}, u32[]{:S(2)}, u32[]{:S(2)}) collective-permute-start(f32[2,64,4096]{2,1,0:T(8,128)S(1)} %add.5383), channel_id=1, source_target_pairs={{0,2},{1,3},{2,0},{3,1},{4,6},{5,7},{6,4},{7,5},{8,10},{9,11},{10,... | collective-permute-start | bytes 6291464 | tf_op jit(solution)/shard_map/ppermute | solution.py:26
  444.4 48.4 %collective-permute-start.8 = (f32[2,64,4096]{2,1,0:T(8,128)S(1)}, f32[2,64,4096]{2,1,0:T(8,128)S(1)}, u32[]{:S(2)}, u32[]{:S(2)}) collective-permute-start(f32[2,64,4096]{2,1,0:T(8,128)S(1)} %pad_maximum_fusion.1), channel_id=1, source_target_pairs={{0,4},{1,5},{2,6},{3,7},{4,0},{5,1},{6,2},{7,3},{8,12},{9,13},{10,... | collective-permute-start | bytes 6291464 | tf_op jit(solution)/shard_map/ppermute | solution.py:26
  492.8 1.3 copy-start
  495.8 46.5 %collective-permute-start.9 = (f32[2,64,4096]{2,1,0:T(8,128)}, f32[2,64,4096]{2,1,0:T(8,128)}, u32[]{:S(2)}, u32[]{:S(2)}) collective-permute-start(f32[2,64,4096]{2,1,0:T(8,128)} %fusion.457), channel_id=1, source_target_pairs={{0,8},{1,9},{2,10},{3,11},{4,12},{5,13},{6,14},{7,15},{8,0},{9,1},... | collective-permute-start | bytes 6291464 | tf_op jit(solution)/shard_map/ppermute | solution.py:26
  544.7 15.1 %copy-start.3 = (f32[2,64,4096]{2,1,0:T(8,128)S(1)}, f32[2,64,4096]{2,1,0:T(8,128)}, u32[]{:S(2)}) copy-start(f32[2,64,4096]{2,1,0:T(8,128)} %custom-call.4) | copy-start | bytes 6291460
  572.7 1.3 copy-start.4
